TPU v7x, 32 devices: a whole 2x2x4 slice. The times are simulated.
32 devices in a mesh: dom: 16 (over z, y, x), orb: 2 (over core).
Axes of the slice: x: 2, y: 2, z: 4, core: 2. Of those that a mesh axis runs over, the one named last changes fastest.
Arguments:
- orbitals: bfloat16 [768, 64, 512], P('dom', 'orb'), may hold values from -6 to 6
- adjoint_source: bfloat16 [768, 64, 512], P('dom', 'orb'), may hold values from -6 to 6
- eigenvalues: float32 [64], P('orb'), may hold values from -1 to -0.25
- cell_scale: float32 [768], P('dom'), may hold values from 0.4 to 1.6
- base_potential: float32 [768, 512], P('dom'), may hold values from 0.5 to 1.5
- stiffness: bfloat16 [512, 512], replicated, may hold values from -1.5 to 1.5, as said below
- face_perm: int32 [768, 64], P('dom'), may hold values from 0 to 63, each once within a row
- restrict: bfloat16 [512, 64], replicated, may hold values from -0.25 to 0.25
- prolong: bfloat16 [64, 512], replicated, may hold values from -0.75 to 0.75
- owner: int32 [768, 1], P('dom'), may hold values from 0 to 15; in each aligned block of 48 rows (0 to 47, 48 to 95, ...) at most 6 rows name the same one
- pot_slot: int32 [768], P('dom'), may hold values from 0 to 63
- potential: float32 [1024, 64], P('dom'), may hold values from -6 to 6
Outputs:
- adjoint: bfloat16 [768, 64, 512], P('dom', 'orb')
- updated: float32 [1024, 64], P('dom')
- applied: bfloat16 [768, 64, 512], P('dom', 'orb')
Inputs may be any that keep to these rules, and one draw needn't show every extreme that they name: In the rows of one device no owner is named by more than 6 cells. `face_perm`: each row is a permutation. `stiffness`: symmetric.
All inputs are finite; a program needn't handle non-finite values.
Results may differ from a plain program's by a relative error of at most 0.0027.
Values sent between devices are 32-bit elements; how exact they have to be, the bound alone decides.
A program may use at most 64 MiB of HBM per device.

v0:
```python
import jax
import jax.numpy as jnp
from jax import lax
from jax.sharding import PartitionSpec as P

ITERS = 4


relax = 0.25
step_rate = 0.1


def padded_2(block, sides, width):
    for axis, dim in sides:
        count = lax.axis_size(axis)
        forward = [(i, i + 1) for i in range(count - 1)]
        backward = [(target, source) for source, target in forward]
        low = lax.ppermute(
            lax.slice_in_dim(block, block.shape[dim] - width, None, axis=dim), axis, forward
        )
        high = lax.ppermute(lax.slice_in_dim(block, 0, width, axis=dim), axis, backward)
        block = jnp.concatenate([low, block, high], axis=dim)
    return block


def local(
    orbitals,
    adjoint_source,
    eigenvalues,
    cell_scale,
    base_potential,
    stiffness,
    face_perm,
    restrict,
    prolong,
    owner,
    pot_slot,
    potential,
):
    nodes = stiffness.shape[0]
    faces = face_perm.shape[1]
    pot_rows = potential.shape[0]
    n_domains = lax.axis_size("dom")
    cell_count = owner.shape[0]
    capacity = 2 * ((cell_count + n_domains - 1) // n_domains)
    onehot = (face_perm[:, :, None] == jnp.arange(faces, dtype=jnp.int32)[None, None, :]).astype(
        jnp.float32
    )

    def assemble_local(partial_sum):
        left_face = partial_sum[:, :, :faces]
        right_face = partial_sum[:, :, nodes - faces :]
        sent_right = jnp.einsum("ckj,cok->coj", onehot, right_face, precision=lax.Precision.HIGHEST)
        boundary = jnp.stack([left_face[0], sent_right[-1]], 0)
        padded = padded_2(boundary, (("dom", 0),), 1)
        left_next = jnp.concatenate([left_face[1:], padded[3][None]], 0)
        add_right = jnp.einsum("ckj,coj->cok", onehot, left_next, precision=lax.Precision.HIGHEST)
        add_left = jnp.concatenate([padded[0][None], sent_right[:-1]], 0)
        return jnp.concatenate(
            [
                left_face + add_left,
                partial_sum[:, :, faces : nodes - faces],
                right_face + add_right,
            ],
            2,
        )

    def operator(values_bf, values_full, shift):
        kinetic = jnp.dot(
            values_bf.reshape(-1, nodes), stiffness, preferred_element_type=jnp.float32
        ).reshape(values_full.shape)
        return assemble_local(cell_scale[:, None, None] * kinetic + shift * values_full)

    source = adjoint_source.astype(jnp.float32)
    shift = base_potential[:, None, :] - eigenvalues[None, :, None]
    iterate = relax * source
    for step_index in range(ITERS):
        image = operator(iterate.astype(jnp.bfloat16), iterate, shift)
        iterate = iterate + relax * (source - image)
    adjoint = iterate.astype(jnp.bfloat16)
    partial_density = jnp.sum(orbitals.astype(jnp.float32) * iterate, axis=1)
    restrict_full = restrict.astype(jnp.float32)
    density_term = lax.psum(partial_density, "orb")
    projected = jnp.dot(density_term, restrict_full, precision=lax.Precision.HIGHEST)
    coarse_cols = projected.shape[1]
    dest_owner = owner[:, 0]
    owner_hot = (dest_owner[:, None] == jnp.arange(n_domains, dtype=jnp.int32)[None, :]).astype(
        jnp.int32
    )
    earlier = jnp.cumsum(owner_hot, axis=0) - owner_hot
    rank_within = jnp.sum(earlier * owner_hot, axis=1)
    slot_index = dest_owner * capacity + rank_within
    send_hot_int = (
        slot_index[None, :] == jnp.arange(n_domains * capacity, dtype=jnp.int32)[:, None]
    ).astype(jnp.int32)
    send_hot = send_hot_int.astype(jnp.float32)
    send_values = jnp.dot(send_hot, projected, precision=lax.Precision.HIGHEST).reshape(
        n_domains, capacity, coarse_cols
    )
    send_ids = (jnp.sum(send_hot_int * (pot_slot + 1)[None, :], axis=1) - 1).reshape(
        n_domains, capacity
    )
    recv_values, recv_ids = (
        lax.all_to_all(send_values, "dom", split_axis=0, concat_axis=0, tiled=True),
        lax.all_to_all(send_ids, "dom", split_axis=0, concat_axis=0, tiled=True),
    )
    recv_hot = (
        recv_ids.reshape(-1)[None, :] == jnp.arange(pot_rows, dtype=jnp.int32)[:, None]
    ).astype(jnp.float32)
    summed = jnp.dot(
        recv_hot, recv_values.reshape(-1, coarse_cols), precision=lax.Precision.HIGHEST
    )
    updated = potential - step_rate * summed
    back_values = jnp.dot(recv_hot.T, updated, precision=lax.Precision.HIGHEST).reshape(
        n_domains, capacity, coarse_cols
    )
    returned = lax.all_to_all(back_values, "dom", split_axis=0, concat_axis=0, tiled=True)
    cell_pot = jnp.dot(
        send_hot.T, returned.reshape(-1, coarse_cols), precision=lax.Precision.HIGHEST
    )
    node_potential = jnp.dot(cell_pot, prolong.astype(jnp.float32), precision=lax.Precision.HIGHEST)
    shift_new = (base_potential + node_potential)[:, None, :]
    applied = operator(orbitals, orbitals.astype(jnp.float32), shift_new).astype(jnp.bfloat16)
    return (adjoint, updated, applied)


def solution(mesh):
    in_specs = (
        P("dom", "orb", None),
        P("dom", "orb", None),
        P("orb"),
        P("dom"),
        P("dom", None),
        P(),
        P("dom", None),
        P(),
        P(),
        P("dom", None),
        P("dom"),
        P("dom", None),
    )
    out_specs = (P("dom", "orb", None), P("dom", None), P("dom", "orb", None))
    return jax.shard_map(local, mesh=mesh, in_specs=in_specs, out_specs=out_specs, check_vma=False)
```

profile of v0, /device:TPU:0, one launch (start us, length us, event | category | flops | bytes accessed | tf_op | source)
XLA Modules:
  0.0 149.0 jit_solution(11445277540518210424)
XLA Ops:
  7.3 1.0 copy-done
  8.2 3.2 %fusion.11 = f32[48,32,512]{2,1,0:T(8,128)S(1)} fusion(bf16[48,32,512]{2,1,0:T(8,128)(2,1)} %param.13, f32[32]{0:T(128)} %param.14, f32[48,512]{1,0:T(8,128)} %param.16, f32[48]{0:T(128)} %param.15, bf16[512,512]{1,0:T(8,128)(2,1)S(1)} %copy-done), kind=kOutput, calls=%fused_computation.22 | convolution fusion | flops 812384256 | bytes 5341504 | tf_op jit(solution)/shard_map/dot_general | solution.py:69
  11.4 1.3 collective-permute-start.1
  13.0 1.8 %fusion.28 = f32[48,32,64]{2,1,0:T(8,128)S(1)} fusion(s32[48,64]{1,0:T(8,128)S(1)} %copy-done.4, f32[48,32,512]{2,1,0:T(8,128)S(1)} %fusion.11), kind=kOutput, calls=%fused_computation.41 | convolution fusion | flops 75694080 | bytes 1204224 | tf_op jit(solution)/shard_map/ckj,cok->coj/dot_general | solution.py:53
  14.8 5.2 %collective-permute-start = (f32[1,32,64]{2,1,0:T(8,128)S(1)}, f32[1,32,64]{2,1,0:T(8,128)S(1)}, u32[]{:S(2)}, u32[]{:S(2)}) collective-permute-start(f32[1,32,64]{2,1,0:T(8,128)S(1)} %slice.153), channel_id=1, source_target_pairs={{0,2},{2,4},{4,6},{6,8},{8,10},{10,12},{12,14},{14,16},{16,18},{18... | collective-permute-start | bytes 24584 | tf_op jit(solution)/shard_map/ppermute | solution.py:18
  20.5 1.2 slice.156
  21.8 2.7 %slice.155 = f32[48,32,384]{2,1,0:T(8,128)S(1)} slice(f32[48,32,512]{2,1,0:T(8,128)} %copy-done.1), slice={[0:48], [0:32], [64:448]} | slice | bytes 4718592 | tf_op jit(solution)/shard_map/slice | solution.py:62
  24.6 1.5 fusion.30
  26.2 2.8 %fusion.12 = f32[48,32,512]{2,1,0:T(8,128)S(1)} fusion(f32[32]{0:T(128)S(1)} %copy-done.13, f32[48,512]{1,0:T(8,128)S(1)} %copy-done.7, f32[48]{0:T(128)S(1)} %copy-done.14, f32[48,32,64]{2,1,0:T(8,128)S(1)} %fusion.30, f32[48,32,384]{2,1,0:T(8,128)S(1)} %slice.155, f32[48,32,64]{2,1,0:T(8,128)S(1)} %slice_add_fusion.4, ...), kind=kOutput, calls=%fused_computation.23 | convolution fusion | flops 820248576 | bytes 8487232 | tf_op jit(solution)/shard_map/dot_general | solution.py:69
  29.0 1.3 collective-permute-start.3
  30.3 1.8 %fusion.26 = f32[48,32,64]{2,1,0:T(8,128)S(1)} fusion(s32[48,64]{1,0:T(8,128)S(1)} %copy-done.4, f32[48,32,512]{2,1,0:T(8,128)S(1)} %fusion.12), kind=kOutput, calls=%fused_computation.39 | convolution fusion | flops 75694080 | bytes 1204224 | tf_op jit(solution)/shard_map/ckj,cok->coj/dot_general | solution.py:53
  32.3 0.7 slice.162
  33.0 5.4 %collective-permute-start.2 = (f32[1,32,64]{2,1,0:T(8,128)S(1)}, f32[1,32,64]{2,1,0:T(8,128)S(1)}, u32[]{:S(2)}, u32[]{:S(2)}) collective-permute-start(f32[1,32,64]{2,1,0:T(8,128)S(1)} %slice.160), channel_id=1, source_target_pairs={{0,2},{2,4},{4,6},{6,8},{8,10},{10,12},{12,14},{14,16},{16,18},{18... | collective-permute-start | bytes 24584 | tf_op jit(solution)/shard_map/ppermute | solution.py:18
  38.5 1.4 fusion.31
  40.1 2.8 %fusion.6 = f32[48,32,512]{2,1,0:T(8,128)S(1)} fusion(bf16[48,32,512]{2,1,0:T(8,128)(2,1)S(1)} %copy-done.3, f32[48,32,64]{2,1,0:T(8,128)S(1)} %fusion.31, f32[48,32,384]{2,1,0:T(8,128)S(1)} %slice.162, f32[48,32,64]{2,1,0:T(8,128)S(1)} %slice_add_fusion.3, f32[48,32,64]{2,1,0:T(8,128)S(1)} %fusion.30, f32[48,32,384]{2,1,0:T(8,128)S(1)} %slice.155, ...), kind=kLoop, calls=%fused_computation.17 | loop fusion | flops 9437184 | bytes 11010048 | tf_op jit(solution)/shard_map/add | solution.py:79
  43.0 1.1 fusion.13
  44.1 1.5 collective-permute-start.5
  45.6 1.8 %fusion.24 = f32[48,32,64]{2,1,0:T(8,128)S(1)} fusion(s32[48,64]{1,0:T(8,128)S(1)} %copy-done.4, f32[48,32,512]{2,1,0:T(8,128)S(1)} %fusion.13), kind=kOutput, calls=%fused_computation.37 | convolution fusion | flops 75694080 | bytes 1204224 | tf_op jit(solution)/shard_map/ckj,cok->coj/dot_general | solution.py:53
  47.6 0.7 slice.169
  48.2 5.4 %collective-permute-start.4 = (f32[1,32,64]{2,1,0:T(8,128)S(1)}, f32[1,32,64]{2,1,0:T(8,128)S(1)}, u32[]{:S(2)}, u32[]{:S(2)}) collective-permute-start(f32[1,32,64]{2,1,0:T(8,128)S(1)} %slice.167), channel_id=1, source_target_pairs={{0,2},{2,4},{4,6},{6,8},{8,10},{10,12},{12,14},{14,16},{16,18},{18... | collective-permute-start | bytes 24584 | tf_op jit(solution)/shard_map/ppermute | solution.py:18
  53.7 1.5 fusion.32
  55.3 2.5 %fusion.14 = f32[48,32,512]{2,1,0:T(8,128)S(1)} fusion(f32[32]{0:T(128)S(1)} %copy-done.13, f32[48,512]{1,0:T(8,128)S(1)} %copy-done.7, f32[48]{0:T(128)S(1)} %copy-done.14, bf16[512,512]{1,0:T(8,128)(2,1)S(1)} %copy-done, f32[48,32,512]{2,1,0:T(8,128)S(1)} %fusion.6, f32[48,32,64]{2,1,0:T(8,128)S(1)} %fusion.32, f32[48,32,384]{2,1,0:T(8,128)S(1)} %slice.169, ...), kind=kOutput, calls=%fused_computation.25 | convolution fusion | flops 818675712 | bytes 11632960 | tf_op jit(solution)/shard_map/dot_general | solution.py:69
  57.8 1.3 collective-permute-start.7
  59.1 1.8 %fusion.22 = f32[48,32,64]{2,1,0:T(8,128)S(1)} fusion(s32[48,64]{1,0:T(8,128)S(1)} %copy-done.4, f32[48,32,512]{2,1,0:T(8,128)S(1)} %fusion.14), kind=kOutput, calls=%fused_computation.35 | convolution fusion | flops 75694080 | bytes 1204224 | tf_op jit(solution)/shard_map/ckj,cok->coj/dot_general | solution.py:53
  61.1 0.7 slice.176
  61.8 5.8 %collective-permute-start.6 = (f32[1,32,64]{2,1,0:T(8,128)S(1)}, f32[1,32,64]{2,1,0:T(8,128)S(1)}, u32[]{:S(2)}, u32[]{:S(2)}) collective-permute-start(f32[1,32,64]{2,1,0:T(8,128)S(1)} %slice.174), channel_id=1, source_target_pairs={{0,2},{2,4},{4,6},{6,8},{8,10},{10,12},{12,14},{14,16},{16,18},{18... | collective-permute-start | bytes 24584 | tf_op jit(solution)/shard_map/ppermute | solution.py:18
  67.6 1.5 fusion.33
  69.3 4.5 %fusion.2 = (f32[48,512]{1,0:T(8,128)}, bf16[48,32,512]{2,1,0:T(8,128)(2,1)}) fusion(bf16[48,32,512]{2,1,0:T(8,128)(2,1)S(1)} %copy-done.5, f32[48,32,64]{2,1,0:T(8,128)S(1)} %fusion.33, f32[48,32,384]{2,1,0:T(8,128)S(1)} %slice.176, f32[48,32,64]{2,1,0:T(8,128)S(1)} %slice_add_fusion.1, f32[48,32,512]{2,1,0:T(8,128)S(1)} %fusion.6, ...), kind=kLoop, calls=%fused_computation.13 | loop fusion | flops 11771904 | bytes 14254080 | tf_op jit(solution)/shard_map/reduce_sum | solution.py:81
  73.9 0.7 sub.46
  74.5 13.0 %all-to-all-start = ((s32[16,1,6]{2,1,0:T(1,128)}), s32[16,1,6]{2,1,0:T(1,128)S(1)}, u32[]{:S(2)}, u32[]{:S(2)}) async-start(s32[16,1,6]{2,1,0:T(1,128)} %bitcast.2), calls=%async_computation | async-start | bytes 16384 | tf_op jit(solution)/shard_map/all_to_all | solution.py:105
  87.5 11.7 %all-reduce.2.cloned.1.call-done = f32[48,512]{1,0:T(8,128)} async-done(((f32[48,512]{1,0:T(8,128)}), f32[48,512]{1,0:T(8,128)}) %all-reduce.2.cloned.1.call-update) | async-done | bytes 98320 | tf_op jit(solution)/shard_map/psum | solution.py:83
  99.2 1.1 fusion.96
  100.6 0.7 reshape.84
  101.3 6.8 %all-to-all-start.1 = ((f32[16,1,384]{2,1,0:T(1,128)}), f32[16,1,384]{2,1,0:T(1,128)S(1)}, u32[]{:S(2)}, u32[]{:S(2)}) async-start(f32[16,1,384]{2,1,0:T(1,128)} %reshape.84), calls=%async_computation.1 | async-start | bytes 49152 | tf_op jit(solution)/shard_map/all_to_all | solution.py:104
  108.2 0.5 broadcast.66
  108.7 0.7 reduce.3
  109.4 6.1 %all-to-all-done.1 = f32[16,1,384]{2,1,0:T(1,128)S(1)} async-done(((f32[16,1,384]{2,1,0:T(1,128)}), f32[16,1,384]{2,1,0:T(1,128)S(1)}, u32[]{:S(2)}, u32[]{:S(2)}) %all-to-all-start.1) | async-done | bytes 24608 | tf_op jit(solution)/shard_map/all_to_all | solution.py:104
  115.5 0.5 broadcast.68
  116.0 0.7 reduce.4
  117.4 9.9 %all_to_all.16 = f32[16,1,384]{2,1,0:T(1,128)S(1)} all-to-all(f32[16,1,384]{2,1,0:T(1,128)S(1)} %reshape.86), channel_id=1, replica_groups=mesh['dom'=16,'orb'=2] {'dom'}, dimensions={0} | all-to-all | bytes 49152 | tf_op jit(solution)/shard_map/all_to_all | solution.py:117
  127.3 0.7 reduce.5
  128.5 1.0 fusion.3
  129.6 1.5 %collective-permute-start.9 = (f32[1,32,64]{2,1,0:T(8,128)S(1)}, f32[1,32,64]{2,1,0:T(8,128)S(1)}, u32[]{:S(2)}, u32[]{:S(2)}) collective-permute-start(f32[1,32,64]{2,1,0:T(8,128)S(1)} %slice.185), channel_id=1, source_target_pairs={{2,0},{4,2},{6,4},{8,6},{10,8},{12,10},{14,12},{16,14},{18,16},{20... | collective-permute-start | bytes 24584 | tf_op jit(solution)/shard_map/ppermute | solution.py:21
  131.1 1.8 %fusion.20 = f32[48,32,64]{2,1,0:T(8,128)S(1)} fusion(s32[48,64]{1,0:T(8,128)S(1)} %copy-done.4, f32[48,32,512]{2,1,0:T(8,128)S(1)} %fusion.3), kind=kOutput, calls=%fused_computation.33 | convolution fusion | flops 75694080 | bytes 1204224 | tf_op jit(solution)/shard_map/ckj,cok->coj/dot_general | solution.py:53
  133.1 0.4 slice.209
  133.6 4.5 %collective-permute-start.8 = (f32[1,32,64]{2,1,0:T(8,128)S(1)}, f32[1,32,64]{2,1,0:T(8,128)S(1)}, u32[]{:S(2)}, u32[]{:S(2)}) collective-permute-start(f32[1,32,64]{2,1,0:T(8,128)S(1)} %slice.181), channel_id=1, source_target_pairs={{0,2},{2,4},{4,6},{6,8},{8,10},{10,12},{12,14},{14,16},{16,18},{18... | collective-permute-start | bytes 24584 | tf_op jit(solution)/shard_map/ppermute | solution.py:18
  138.1 1.7 %fusion.35 = bf16[48,32,64]{2,1,0:T(8,128)(2,1)S(1)} fusion(f32[1,32,64]{2,1,0:T(8,128)S(1)} %collective-permute-done.9, f32[47,32,64]{2,1,0:T(8,128)S(1)} %slice.184, s32[48,64]{1,0:T(8,128)S(1)} %copy-done.4, f32[48,32,512]{2,1,0:T(8,128)S(1)} %fusion.3), kind=kOutput, calls=%fused_computation.48 | convolution fusion | flops 75988992 | bytes 995328 | tf_op jit(solution)/shard_map/ckj,coj->cok/dot_general | solution.py:57
  140.0 2.1 %pad_maximum_fusion = bf16[48,32,512]{2,1,0:T(8,128)(2,1)} fusion(bf16[48,32,64]{2,1,0:T(8,128)(2,1)S(1)} %fusion.35, bf16[48,32,384]{2,1,0:T(8,128)(2,1)S(1)} %slice.209, bf16[48,32,64]{2,1,0:T(8,128)(2,1)S(1)} %fusion.38), kind=kLoop, calls=%fused_computation.27 | loop fusion | flops 4718592 | bytes 3145728 | tf_op jit(solution)/shard_map/concatenate | solution.py:59
  (86 shorter events, 3.9 us)
Async XLA Ops:
  7.2 1.0 copy-start
  7.2 5.8 %copy-start.4 = (s32[48,64]{1,0:T(8,128)S(1)}, s32[48,64]{1,0:T(8,128)}, u32[]{:S(2)}) copy-start(s32[48,64]{1,0:T(8,128)} %param.18) | copy-start | bytes 36868
  7.2 12.9 %copy-start.12 = (s32[48]{0:T(128)S(1)}, s32[48]{0:T(128)}, u32[]{:S(2)}) copy-start(s32[48]{0:T(128)} %param.22) | copy-start | bytes 580
  7.2 12.9 %copy-start.11 = (s32[48,1]{0,1:T(1,128)S(1)}, s32[48,1]{0,1:T(1,128)}, u32[]{:S(2)}) copy-start(s32[48,1]{0,1:T(1,128)} %param.21) | copy-start | bytes 580
  7.2 92.0 %all-reduce.2.cloned.1.call-start = ((), (), s32[]{:S(2)}) async-start(), calls=%async_computation.3 | async-start | bytes 196608 | tf_op jit(solution)/shard_map/psum | solution.py:83
  11.4 1.6 %copy-start.1 = (f32[48,32,512]{2,1,0:T(8,128)}, f32[48,32,512]{2,1,0:T(8,128)S(1)}, u32[]{:S(2)}) copy-start(f32[48,32,512]{2,1,0:T(8,128)S(1)} %fusion.11) | copy-start | bytes 9437188
  11.4 13.1 %collective-permute-start.1 = (f32[1,32,64]{2,1,0:T(8,128)S(1)}, f32[1,32,64]{2,1,0:T(8,128)S(1)}, u32[]{:S(2)}, u32[]{:S(2)}) collective-permute-start(f32[1,32,64]{2,1,0:T(8,128)S(1)} %slice.157), channel_id=1, source_target_pairs={{2,0},{4,2},{6,4},{8,6},{10,8},{12,10},{14,12},{16,14},{18,16},{20... | collective-permute-start | bytes 24584 | tf_op jit(solution)/shard_map/ppermute | solution.py:21
  14.8 11.2 %collective-permute-start = (f32[1,32,64]{2,1,0:T(8,128)S(1)}, f32[1,32,64]{2,1,0:T(8,128)S(1)}, u32[]{:S(2)}, u32[]{:S(2)}) collective-permute-start(f32[1,32,64]{2,1,0:T(8,128)S(1)} %slice.153), channel_id=1, source_target_pairs={{0,2},{2,4},{4,6},{6,8},{8,10},{10,12},{12,14},{14,16},{16,18},{18... | collective-permute-start | bytes 24584 | tf_op jit(solution)/shard_map/ppermute | solution.py:18
  21.7 2.8 %copy-start.2 = (f32[48,32,512]{2,1,0:T(8,128)S(1)}, f32[48,32,512]{2,1,0:T(8,128)}, u32[]{:S(2)}) copy-start(f32[48,32,512]{2,1,0:T(8,128)} %copy-done.1) | copy-start | bytes 9437188
  24.5 1.7 %copy-start.3 = (bf16[48,32,512]{2,1,0:T(8,128)(2,1)S(1)}, bf16[48,32,512]{2,1,0:T(8,128)(2,1)}, u32[]{:S(2)}) copy-start(bf16[48,32,512]{2,1,0:T(8,128)(2,1)} %param.13) | copy-start | bytes 4718596
  24.5 1.7 %copy-start.7 = (f32[48,512]{1,0:T(8,128)S(1)}, f32[48,512]{1,0:T(8,128)}, u32[]{:S(2)}) copy-start(f32[48,512]{1,0:T(8,128)} %param.16) | copy-start | bytes 294916
  24.5 1.7 %copy-start.13 = (f32[32]{0:T(128)S(1)}, f32[32]{0:T(128)}, u32[]{:S(2)}) copy-start(f32[32]{0:T(128)} %param.14) | copy-start | bytes 388
  24.5 1.7 %copy-start.14 = (f32[48]{0:T(128)S(1)}, f32[48]{0:T(128)}, u32[]{:S(2)}) copy-start(f32[48]{0:T(128)} %param.15) | copy-start | bytes 580
  29.0 9.4 %collective-permute-start.3 = (f32[1,32,64]{2,1,0:T(8,128)S(1)}, f32[1,32,64]{2,1,0:T(8,128)S(1)}, u32[]{:S(2)}, u32[]{:S(2)}) collective-permute-start(f32[1,32,64]{2,1,0:T(8,128)S(1)} %slice.164), channel_id=1, source_target_pairs={{2,0},{4,2},{6,4},{8,6},{10,8},{12,10},{14,12},{16,14},{18,16},{20... | collective-permute-start | bytes 24584 | tf_op jit(solution)/shard_map/ppermute | solution.py:21
  33.0 6.9 %collective-permute-start.2 = (f32[1,32,64]{2,1,0:T(8,128)S(1)}, f32[1,32,64]{2,1,0:T(8,128)S(1)}, u32[]{:S(2)}, u32[]{:S(2)}) collective-permute-start(f32[1,32,64]{2,1,0:T(8,128)S(1)} %slice.160), channel_id=1, source_target_pairs={{0,2},{2,4},{4,6},{6,8},{8,10},{10,12},{12,14},{14,16},{16,18},{18... | collective-permute-start | bytes 24584 | tf_op jit(solution)/shard_map/ppermute | solution.py:18
  44.1 9.6 %collective-permute-start.5 = (f32[1,32,64]{2,1,0:T(8,128)S(1)}, f32[1,32,64]{2,1,0:T(8,128)S(1)}, u32[]{:S(2)}, u32[]{:S(2)}) collective-permute-start(f32[1,32,64]{2,1,0:T(8,128)S(1)} %slice.171), channel_id=1, source_target_pairs={{2,0},{4,2},{6,4},{8,6},{10,8},{12,10},{14,12},{16,14},{18,16},{20... | collective-permute-start | bytes 24584 | tf_op jit(solution)/shard_map/ppermute | solution.py:21
  48.2 6.9 %collective-permute-start.4 = (f32[1,32,64]{2,1,0:T(8,128)S(1)}, f32[1,32,64]{2,1,0:T(8,128)S(1)}, u32[]{:S(2)}, u32[]{:S(2)}) collective-permute-start(f32[1,32,64]{2,1,0:T(8,128)S(1)} %slice.167), channel_id=1, source_target_pairs={{0,2},{2,4},{4,6},{6,8},{8,10},{10,12},{12,14},{14,16},{16,18},{18... | collective-permute-start | bytes 24584 | tf_op jit(solution)/shard_map/ppermute | solution.py:18
  57.8 9.8 %collective-permute-start.7 = (f32[1,32,64]{2,1,0:T(8,128)S(1)}, f32[1,32,64]{2,1,0:T(8,128)S(1)}, u32[]{:S(2)}, u32[]{:S(2)}) collective-permute-start(f32[1,32,64]{2,1,0:T(8,128)S(1)} %slice.178), channel_id=1, source_target_pairs={{2,0},{4,2},{6,4},{8,6},{10,8},{12,10},{14,12},{16,14},{18,16},{20... | collective-permute-start | bytes 24584 | tf_op jit(solution)/shard_map/ppermute | solution.py:21
  61.8 7.5 %copy-start.5 = (bf16[48,32,512]{2,1,0:T(8,128)(2,1)S(1)}, bf16[48,32,512]{2,1,0:T(8,128)(2,1)}, u32[]{:S(2)}) copy-start(bf16[48,32,512]{2,1,0:T(8,128)(2,1)} %param.12) | copy-start | bytes 4718596
  61.8 7.3 %collective-permute-start.6 = (f32[1,32,64]{2,1,0:T(8,128)S(1)}, f32[1,32,64]{2,1,0:T(8,128)S(1)}, u32[]{:S(2)}, u32[]{:S(2)}) collective-permute-start(f32[1,32,64]{2,1,0:T(8,128)S(1)} %slice.174), channel_id=1, source_target_pairs={{0,2},{2,4},{4,6},{6,8},{8,10},{10,12},{12,14},{14,16},{16,18},{18... | collective-permute-start | bytes 24584 | tf_op jit(solution)/shard_map/ppermute | solution.py:18
  69.3 29.9 %copy-start.8 = (bf16[512,64]{0,1:T(8,128)(2,1)S(1)}, bf16[512,64]{0,1:T(8,128)(2,1)}, u32[]{:S(2)}) copy-start(bf16[512,64]{0,1:T(8,128)(2,1)} %param.19) | copy-start | bytes 196612
  69.3 47.6 %copy-start.10 = (f32[64,64]{1,0:T(8,128)S(1)}, f32[64,64]{1,0:T(8,128)}, u32[]{:S(2)}) copy-start(f32[64,64]{1,0:T(8,128)} %param.23) | copy-start | bytes 49156
  69.3 59.1 %copy-start.9 = (bf16[64,512]{1,0:T(8,128)(2,1)S(1)}, bf16[64,512]{1,0:T(8,128)(2,1)}, u32[]{:S(2)}) copy-start(bf16[64,512]{1,0:T(8,128)(2,1)} %param.20) | copy-start | bytes 196612
  74.5 26.8 %all-to-all-start = ((s32[16,1,6]{2,1,0:T(1,128)}), s32[16,1,6]{2,1,0:T(1,128)S(1)}, u32[]{:S(2)}, u32[]{:S(2)}) async-start(s32[16,1,6]{2,1,0:T(1,128)} %bitcast.2), calls=%async_computation | async-start | bytes 16384 | tf_op jit(solution)/shard_map/all_to_all | solution.py:105
  101.3 14.2 %all-to-all-start.1 = ((f32[16,1,384]{2,1,0:T(1,128)}), f32[16,1,384]{2,1,0:T(1,128)S(1)}, u32[]{:S(2)}, u32[]{:S(2)}) async-start(f32[16,1,384]{2,1,0:T(1,128)} %reshape.84), calls=%async_computation.1 | async-start | bytes 49152 | tf_op jit(solution)/shard_map/all_to_all | solution.py:104
  117.0 12.6 %copy-start.6 = (f32[64,64]{1,0:T(8,128)}, f32[64,64]{1,0:T(8,128)S(1)}, u32[]{:S(2)}) copy-start(f32[64,64]{1,0:T(8,128)S(1)} %fusion.36) | copy-start | bytes 49156
  129.6 8.5 %collective-permute-start.9 = (f32[1,32,64]{2,1,0:T(8,128)S(1)}, f32[1,32,64]{2,1,0:T(8,128)S(1)}, u32[]{:S(2)}, u32[]{:S(2)}) collective-permute-start(f32[1,32,64]{2,1,0:T(8,128)S(1)} %slice.185), channel_id=1, source_target_pairs={{2,0},{4,2},{6,4},{8,6},{10,8},{12,10},{14,12},{16,14},{18,16},{20... | collective-permute-start | bytes 24584 | tf_op jit(solution)/shard_map/ppermute | solution.py:21
  133.6 6.3 %collective-permute-start.8 = (f32[1,32,64]{2,1,0:T(8,128)S(1)}, f32[1,32,64]{2,1,0:T(8,128)S(1)}, u32[]{:S(2)}, u32[]{:S(2)}) collective-permute-start(f32[1,32,64]{2,1,0:T(8,128)S(1)} %slice.181), channel_id=1, source_target_pairs={{0,2},{2,4},{4,6},{6,8},{8,10},{10,12},{12,14},{14,16},{16,18},{18... | collective-permute-start | bytes 24584 | tf_op jit(solution)/shard_map/ppermute | solution.py:18
Sparse Core Ops, SparseCore 0:
  74.0 25.1 all-reduce.1
where the time goes:
time: 150 us; the launch traced here: 149 us
  starting transfers between devices  53.2 us (35%)
  matrix products  29.3 us (20%)
  waiting for transfers between devices  17.8 us (12%)
  between operations  14.8 us (10%)
  other arithmetic  12.8 us (9%)
  local copies, waits for them, and re-layouts  11.2 us (7%)
  blocking collectives  9.95 us (7%)
    ppermute x5, starting transfers between devices, padded_2(): lax.ppermute(lax.slice_in_dim(block, block.shape[dim] - width, None, axis...  26.5 us
    all_to_all x1, starting transfers between devices, local(): lax.all_to_all(send_ids, 'dom', split_axis=0, concat_axis=0, tiled=True)  13 us
    psum x1, waiting for transfers between devices, local(): density_term = lax.psum(partial_density, 'orb')  11.7 us
    dot_general x5, matrix products, operator(): jnp.dot(values_bf.reshape(-1, nodes), stiffness, preferred_element_type=j...  10.6 us
    all_to_all x1, blocking collectives, local(): lax.all_to_all(back_values, 'dom', split_axis=0, concat_axis=0, tiled=True)  9.95 us
    dot_general x5, matrix products, assemble_local(): jnp.einsum('ckj,cok->coj', onehot, right_face, precision=lax.Precision.HI...  9.01 us
    dot_general x5, matrix products, assemble_local(): jnp.einsum('ckj,coj->cok', onehot, left_next, precision=lax.Precision.HIG...  7.53 us
    ppermute x5, starting transfers between devices, padded_2(): lax.ppermute(lax.slice_in_dim(block, 0, width, axis=dim), axis, backward)  6.86 us
  transfers between devices with their start and end apart: 13, of which 2 were waited for; matrix products, arithmetic and copies ran while one was open for 19% of the time, Pallas kernels for 0%

commit v1 on v0

v1 whole, which is shorter than its diff:
```python
import functools

import jax
import jax.numpy as jnp
from jax import lax
from jax.experimental import pallas as pl
from jax.experimental.pallas import tpu as pltpu
from jax.sharding import PartitionSpec as P

ITERS = 4


relax = 0.25
step_rate = 0.1

LANES = 128
F32 = jnp.float32
BF16 = jnp.bfloat16


def split(x):
    hi = x.astype(BF16)
    return hi, (x - hi.astype(F32)).astype(BF16)


def dot(a, b):
    return jnp.dot(a, b, preferred_element_type=F32)


def dot_first(a, b):
    return lax.dot_general(a, b, (((0,), (0,)), ((), ())), preferred_element_type=F32)


def kernel(
    n,
    ranks,
    psi,
    src,
    eig,
    scale,
    base,
    stiff,
    idx,
    early,
    restrict,
    prolong,
    pot,
    adj,
    upd,
    app,
    it,
    kin,
    face0,
    face3,
    dens,
    tx_l,
    tx_r,
    rx_l,
    rx_r,
    ex_tl,
    ex_tr,
    ex_l,
    ex_r,
    early_all,
    rows_all,
    own,
    mt_lo,
    mt_hi,
    tcols,
    tturn,
    packed,
    packed_in,
    node,
    hs_l,
    hs_r,
    hr_l,
    hr_r,
    xs,
    xr,
    es,
    er,
    ps,
    pr,
    ws,
    wr,
):
    cells, orbs, nodes = psi.shape
    half = cells // 2
    prow = pot.shape[0]
    phalf = prow // 2
    coarse = pot.shape[1]
    last = nodes - LANES
    d = lax.axis_index("dom")
    r = lax.axis_index("orb")
    barrier = pltpu.get_barrier_semaphore()

    def greet_dom(k, carry):
        pl.semaphore_signal(barrier, inc=1, device_id={"dom": lax.rem(d + k, n)}, device_id_type=pl.DeviceIdType.MESH)
        return carry

    def greet_orb(k, carry):
        pl.semaphore_signal(barrier, inc=1, device_id={"orb": lax.rem(r + k, ranks)}, device_id_type=pl.DeviceIdType.MESH)
        return carry

    lax.fori_loop(1, n, greet_dom, 0)
    lax.fori_loop(1, ranks, greet_orb, 0)

    def send(source, target, s, t, where):
        return pltpu.make_async_remote_copy(
            src_ref=source,
            dst_ref=target,
            send_sem=s,
            recv_sem=t,
            device_id=where,
            device_id_type=pl.DeviceIdType.MESH,
        )

    right = {"dom": jnp.minimum(d + 1, n - 1)}
    left = {"dom": jnp.maximum(d - 1, 0)}
    has_right = d < n - 1
    has_left = d > 0

    def to_left(t):
        return send(tx_l.at[t], rx_r.at[t], hs_l.at[t], hr_r.at[t], left)

    def to_right(t):
        return send(tx_r.at[t], rx_l.at[t], hs_r.at[t], hr_l.at[t], right)

    x_left = send(ex_tl, ex_r, xs.at[0], xr.at[0], left)
    x_right = send(ex_tr, ex_l, xs.at[1], xr.at[1], right)

    def early_copy(k):
        return send(early, early_all.at[d], es.at[k], er.at[k], {"dom": lax.rem(d + k, n)})

    def rows_copy(k):
        return send(own, rows_all.at[d], ps.at[k], pr.at[k], {"dom": lax.rem(d + k, n)})

    def rank_copy(k):
        return send(packed, packed_in.at[k], ws.at[k], wr.at[k], {"orb": lax.rem(r + k, ranks)})

    lane = lax.broadcasted_iota(jnp.int32, (orbs, LANES), 1)
    low = lane < LANES // 2

    def turned(x, row):
        return jnp.take_along_axis(x, jnp.broadcast_to(row, (orbs, LANES)), axis=1)

    group = 8 if cells % 8 == 0 else 1

    def init(c, carry):
        it[c] = relax * src[c].astype(F32)
        return carry

    lax.fori_loop(0, cells, init, 0, unroll=4)

    def apply_group(g, carry):
        block = psi[pl.ds(g * group, group)].astype(F32).reshape(group * orbs, nodes).astype(BF16)
        product = dot(block, stiff[...])
        for k in range(group):
            c = g * group + k
            part = product[k * orbs : (k + 1) * orbs]
            kin[c] = scale[c] * part + base[pl.ds(c, 1), :] * psi[c].astype(F32)
        return carry

    def step_group(g, carry):
        block = it[pl.ds(g * group, group)].reshape(group * orbs, nodes).astype(BF16)
        product = dot(block, stiff[...])
        for k in range(group):
            c = g * group + k
            value = it[c]
            part = scale[c] * product[k * orbs : (k + 1) * orbs] + (base[pl.ds(c, 1), :] - eig[...]) * value
            it[c] = value + relax * (src[c].astype(F32) - part)
            face0[c] = part[:, :LANES]
            face3[c] = part[:, last:]
        return carry

    def inner_face(c, carry):
        y = turned(jnp.where(low, face0[c + 1], face3[c]), idx[pl.ds(c, 1), :])
        it[c + 1, :, :LANES] = it[c + 1, :, :LANES] - relax * jnp.where(low, y, 0.0)
        it[c, :, last:] = it[c, :, last:] - relax * jnp.where(low, 0.0, y)
        return carry

    end = cells - 1
    shares = -(-(n - 1) // max(1, ITERS - 1))
    for t in range(ITERS):
        edge = it[0]
        tx_l[t] = scale[0] * dot(edge.astype(BF16), stiff[:, :LANES]) + (base[0:1, :LANES] - eig[...]) * edge[:, :LANES]
        edge = it[end]
        part = scale[end] * dot(edge.astype(BF16), stiff[:, last:]) + (base[end : end + 1, last:] - eig[...]) * edge[:, last:]
        tx_r[t] = turned(part, idx[end : end + 1, :])
        if t == 0:
            pl.semaphore_wait(barrier, n - 1 + ranks - 1)

        @pl.when(has_left)
        def _():
            to_left(t).start()

        @pl.when(has_right)
        def _():
            to_right(t).start()

        def send_early(k, carry):
            early_copy(k).start()
            return carry

        lax.fori_loop(min(n, 1 + t * shares), min(n, 1 + (t + 1) * shares), send_early, 0)
        lax.fori_loop(0, cells // group, step_group, 0)
        lax.fori_loop(0, end, inner_face, 0, unroll=2)
        if t == 0:
            lax.fori_loop(0, cells // group, apply_group, 0)
            ex_tl[:orbs] = kin[0, :, :LANES]
            ex_tl[orbs:] = psi[0].astype(F32)[:, :LANES]
            ex_tr[:orbs] = kin[end, :, last:]
            ex_tr[orbs : 2 * orbs] = psi[end].astype(F32)[:, last:]
            ex_tr[2 * orbs :] = jnp.broadcast_to(idx[end : end + 1, :], (8, LANES)).astype(F32)

            @pl.when(has_left)
            def _():
                x_left.start()

            @pl.when(has_right)
            def _():
                x_right.start()

        @pl.when(has_left)
        def _():
            to_right(t).wait_recv()
            it[0, :, :LANES] = it[0, :, :LANES] - relax * jnp.where(low, rx_l[t], 0.0)

        @pl.when(has_right)
        def _():
            to_left(t).wait_recv()
            y = turned(rx_r[t], idx[end : end + 1, :])
            it[end, :, last:] = it[end, :, last:] - relax * jnp.where(low, 0.0, y)

    def finish(c, carry):
        dens[pl.ds(c, 1), :] = jnp.sum(psi[c].astype(F32) * it[c], axis=0, keepdims=True)
        return carry

    lax.fori_loop(0, cells, finish, 0, unroll=2)
    d_hi, d_lo = split(dens[...])
    projected = dot(d_hi, restrict[...]) + dot(d_lo, restrict[...])
    rows = jnp.concatenate([projected[:half], projected[half:]], axis=1)
    own[...] = rows
    rows_all[d] = rows

    def send_rows(k, carry):
        rows_copy(k).start()
        return carry

    lax.fori_loop(1, n, send_rows, 0)

    def store(c, carry):
        adj[c] = it[c].astype(BF16)
        return carry

    lax.fori_loop(0, cells, store, 0, unroll=2)
    early_all[d] = early[...]

    def wait_early(k, carry):
        early_copy(k).wait()
        return carry

    lax.fori_loop(1, n, wait_early, 0)

    tcols[...] = jnp.zeros_like(tcols)

    def take_row(e, carry):
        tcols[pl.ds(e, 1), :] = early_all[e, phalf : phalf + 1, :]
        return carry

    lax.fori_loop(0, n, take_row, 0)
    tturn[...] = jnp.transpose(tcols[...])
    lane1 = lax.broadcasted_iota(jnp.int32, (1, LANES), 1)

    def spot(e, at):
        row = early_all[e, phalf : phalf + 1, :]
        return jnp.sum(jnp.where(lane1 == at, row, 0.0), axis=1, keepdims=True)

    wanted = early_all[d, phalf : phalf + 1, :]
    wanted = jnp.where(lane1 == cells, spot(jnp.maximum(d - 1, 0), cells - 1), wanted)
    wanted = jnp.where(lane1 == cells + 1, spot(jnp.minimum(d + 1, n - 1), 0), wanted)
    wanted = jnp.where(lane1 >= prow, (d * prow + lane1 - prow).astype(F32), wanted)
    for e in range(n):
        rows_e = pl.ds(e * half, half)
        mt_lo[rows_e, :] = (tturn[:half, e : e + 1] == wanted).astype(F32)
        mt_hi[rows_e, :] = (tturn[half : 2 * half, e : e + 1] == wanted).astype(F32)
    wanted_i = wanted.astype(jnp.int32)
    slot = wanted_i % prow
    spread = (wanted_i // prow) * phalf + slot % phalf
    hit = lax.broadcasted_iota(jnp.int32, (n * phalf, LANES), 0) == spread
    table = early_all[:, :phalf, :].reshape(n * phalf, LANES)
    t_hi, t_lo = split(table)
    hit_lo = jnp.where(hit & (slot < phalf), 1.0, 0.0).astype(BF16)
    hit_hi = jnp.where(hit & (slot >= phalf), 1.0, 0.0).astype(BF16)
    pot_rows = dot_first(hit_lo, t_hi) + dot_first(hit_lo, t_lo)
    pot_rows = pot_rows + pltpu.roll(dot_first(hit_hi, t_hi) + dot_first(hit_hi, t_lo), LANES // 2, 1)

    def wait_rows(k, carry):
        rows_copy(k).wait()
        return carry

    lax.fori_loop(1, n, wait_rows, 0)
    g_hi, g_lo = split(rows_all[...].reshape(n * half, LANES))
    m_lo, m_hi = mt_lo[...].astype(BF16), mt_hi[...].astype(BF16)
    total = dot_first(m_lo, g_hi) + dot_first(m_lo, g_lo)
    total = total + pltpu.roll(dot_first(m_hi, g_hi) + dot_first(m_hi, g_lo), LANES // 2, 1)
    lane64 = lax.broadcasted_iota(jnp.int32, (prow, LANES), 1)
    mine = jnp.where(lane64 < coarse, total[:prow], pltpu.roll(total[prow:], LANES // 2, 1))
    packed[...] = mine
    for k in range(1, ranks):
        rank_copy(k).start()
    for k in range(1, ranks):
        rank_copy(k).wait()
        mine = mine + packed_in[k]
    upd[...] = pot[...] - step_rate * pltpu.roll(mine, LANES // 2, 1)[:, :coarse]
    c_hi, c_lo = split((pot_rows[:prow] - step_rate * mine)[:, :coarse])
    node[...] = dot(c_hi, prolong[...]) + dot(c_lo, prolong[...])

    def value0(c):
        return kin[c, :, :LANES] + node[pl.ds(c, 1), :][:, :LANES] * psi[c, :, :LANES].astype(F32)

    def value3(c):
        return kin[c, :, last:] + node[pl.ds(c, 1), :][:, last:] * psi[c, :, last:].astype(F32)

    def middle(c, carry):
        app[c, :, LANES:last] = (
            kin[c, :, LANES:last] + node[pl.ds(c, 1), :][:, LANES:last] * psi[c, :, LANES:last].astype(F32)
        ).astype(BF16)
        return carry

    lax.fori_loop(0, cells, middle, 0, unroll=4)

    def joint(c, carry):
        t0, t3 = value0(c + 1), value3(c)
        y = turned(jnp.where(low, t0, t3), idx[pl.ds(c, 1), :])
        app[c + 1, :, :LANES] = (t0 + jnp.where(low, y, 0.0)).astype(BF16)
        app[c, :, last:] = (t3 + jnp.where(low, 0.0, y)).astype(BF16)
        return carry

    lax.fori_loop(0, end, joint, 0, unroll=2)
    app[0, :, :LANES] = value0(0).astype(BF16)
    app[end, :, last:] = value3(end).astype(BF16)

    @pl.when(has_left)
    def _():
        x_right.wait_recv()
        far = ex_l[:orbs] + node[cells : cells + 1, last:] * ex_l[orbs : 2 * orbs]
        y = turned(far, ex_l[2 * orbs : 2 * orbs + 1].astype(jnp.int32))
        app[0, :, :LANES] = (value0(0) + jnp.where(low, y, 0.0)).astype(BF16)

    @pl.when(has_right)
    def _():
        x_left.wait_recv()
        far = ex_r[:orbs] + node[cells + 1 : cells + 2, :LANES] * ex_r[orbs:]
        y = turned(far, idx[end : end + 1, :])
        app[end, :, last:] = (value3(end) + jnp.where(low, 0.0, y)).astype(BF16)

    @pl.when(has_left)
    def _():
        x_left.wait_send()
        for t in range(ITERS):
            to_left(t).wait_send()

    @pl.when(has_right)
    def _():
        x_right.wait_send()
        for t in range(ITERS):
            to_right(t).wait_send()


def local(
    n,
    ranks,
    orbitals,
    adjoint_source,
    eigenvalues,
    cell_scale,
    base_potential,
    stiffness,
    face_perm,
    restrict,
    prolong,
    owner,
    pot_slot,
    potential,
):
    cells, orbs, nodes = orbitals.shape
    faces = face_perm.shape[1]
    prow, coarse = potential.shape
    count = jnp.arange(faces, dtype=jnp.int32)
    inverse = jnp.sum(jnp.where(face_perm[:, :, None] == count[None, None, :], count[None, :, None], 0), axis=1)
    idx = jnp.concatenate([inverse + faces, face_perm], axis=1)
    target = (owner[:, 0] * prow + pot_slot).astype(F32)
    target = jnp.broadcast_to(jnp.pad(target, (0, LANES - cells))[None], (8, LANES))
    early = jnp.concatenate(
        [jnp.concatenate([potential[: prow // 2], potential[prow // 2 :]], axis=1), target], axis=0
    )
    vmem = pl.BlockSpec(memory_space=pltpu.VMEM)
    smem = pl.BlockSpec(memory_space=pltpu.SMEM)
    dma = pltpu.SemaphoreType.DMA
    half = cells // 2
    face = (orbs, LANES)
    return pl.pallas_call(
        functools.partial(kernel, n, ranks),
        out_shape=(
            jax.ShapeDtypeStruct(orbitals.shape, BF16),
            jax.ShapeDtypeStruct(potential.shape, F32),
            jax.ShapeDtypeStruct(orbitals.shape, BF16),
        ),
        in_specs=[vmem, vmem, vmem, smem, vmem, vmem, vmem, vmem, vmem, vmem, vmem],
        out_specs=(vmem, vmem, vmem),
        scratch_shapes=[
            pltpu.VMEM((cells, orbs, nodes), F32),
            pltpu.VMEM((cells, orbs, nodes), F32),
            pltpu.VMEM((cells,) + face, F32),
            pltpu.VMEM((cells,) + face, F32),
            pltpu.VMEM((cells, nodes), F32),
            pltpu.VMEM((ITERS,) + face, F32),
            pltpu.VMEM((ITERS,) + face, F32),
            pltpu.VMEM((ITERS,) + face, F32),
            pltpu.VMEM((ITERS,) + face, F32),
            pltpu.VMEM((2 * orbs, LANES), F32),
            pltpu.VMEM((2 * orbs + 8, LANES), F32),
            pltpu.VMEM((2 * orbs + 8, LANES), F32),
            pltpu.VMEM((2 * orbs, LANES), F32),
            pltpu.VMEM((n, prow // 2 + 8, LANES), F32),
            pltpu.VMEM((n, half, LANES), F32),
            pltpu.VMEM((half, LANES), F32),
            pltpu.VMEM((n * half, LANES), F32),
            pltpu.VMEM((n * half, LANES), F32),
            pltpu.VMEM((LANES, LANES), F32),
            pltpu.VMEM((LANES, LANES), F32),
            pltpu.VMEM((prow, LANES), F32),
            pltpu.VMEM((ranks, prow, LANES), F32),
            pltpu.VMEM((prow, nodes), F32),
            dma((ITERS,)),
            dma((ITERS,)),
            dma((ITERS,)),
            dma((ITERS,)),
            dma((2,)),
            dma((2,)),
            dma((n,)),
            dma((n,)),
            dma((n,)),
            dma((n,)),
            dma((ranks,)),
            dma((ranks,)),
        ],
        compiler_params=pltpu.CompilerParams(collective_id=0, has_side_effects=True),
    )(
        orbitals,
        adjoint_source,
        eigenvalues[:, None],
        cell_scale,
        base_potential,
        stiffness,
        idx,
        early,
        restrict,
        prolong,
        potential,
    )


def solution(mesh):
    in_specs = (
        P("dom", "orb", None),
        P("dom", "orb", None),
        P("orb"),
        P("dom"),
        P("dom", None),
        P(),
        P("dom", None),
        P(),
        P(),
        P("dom", None),
        P("dom"),
        P("dom", None),
    )
    out_specs = (P("dom", "orb", None), P("dom", None), P("dom", "orb", None))
    step = functools.partial(local, mesh.shape["dom"], mesh.shape["orb"])
    return jax.shard_map(step, mesh=mesh, in_specs=in_specs, out_specs=out_specs, check_vma=False)
```

time: 150 us -> 53.9 us (0.36)
  starting transfers between devices: 53.2 us -> 0 us
  Pallas kernels: 0 us -> 40.4 us
  matrix products: 29.3 us -> 0 us
  waiting for transfers between devices: 17.8 us -> 0 us
  between operations: 14.8 us -> 0.68 us
  blocking collectives: 9.95 us -> 0 us
  other arithmetic: 12.8 us -> 4.07 us
  local copies, waits for them, and re-layouts: 11.2 us -> 8.29 us
    pallas_call x0 -> x1, Pallas kernels: none -> 40.4 us  [local(): pl.pallas_call(functools.partial(kernel, n, ranks), out_shape=(jax.ShapeD...]
    ppermute x10 -> x0, starting transfers between devices: 33.3 us -> none  [the longest x5 26.5 us: padded_2(): lax.ppermute(lax.slice_in_dim(block, block.shape[dim] - width, None, axis...]
    dot_general x21 -> x0, matrix products: 29.3 us -> none  [the longest x5 10.6 us: operator(): jnp.dot(values_bf.reshape(-1, nodes), stiffness, preferred_element_type=j...]
    all_to_all x2 -> x0, starting transfers between devices: 19.8 us -> none  [the longest x1 13 us: local(): lax.all_to_all(send_ids, 'dom', split_axis=0, concat_axis=0, tiled=True)]
    psum x1 -> x0, waiting for transfers between devices: 11.7 us -> none  [local(): density_term = lax.psum(partial_density, 'orb')]
    all_to_all x1 -> x0, blocking collectives: 9.95 us -> none  [local(): lax.all_to_all(back_values, 'dom', split_axis=0, concat_axis=0, tiled=True)]
    slice x25 -> x1, local copies, waits for them, and re-layouts: 7.05 us -> 0.74 us  [local(): potential[:prow // 2]]
    all_to_all x2 -> x0, waiting for transfers between devices: 6.09 us -> none  [the longest x1 6.09 us: local(): lax.all_to_all(send_values, 'dom', split_axis=0, concat_axis=0, tiled=True)]
  transfers between devices with their start and end apart: 13 -> 0, of which waited for: 2 -> 0; matrix products, arithmetic and copies ran while one was open for 19% -> 0% of each run, Pallas kernels for 0% -> 0%
where the time goes in v1:
time: 53.9 us; the launch traced here: 53.4 us
  Pallas kernels  40.4 us (75%)
  local copies, waits for them, and re-layouts  8.29 us (15%)
  other arithmetic  4.07 us (8%)
  between operations  0.68 us (1%)
    pallas_call x1, Pallas kernels, local(): pl.pallas_call(functools.partial(kernel, n, ranks), out_shape=(jax.ShapeD...  40.4 us
    unnamed x8, local copies, waits for them, and re-layouts  6.21 us
    concatenate x1, other arithmetic, local(): idx = jnp.concatenate([inverse + faces, face_perm], axis=1)  1.43 us
    broadcast_in_dim x1, local copies, waits for them, and re-layouts, local(): eigenvalues[:, None]  1.33 us
    reduce_sum x1, other arithmetic, local(): jnp.sum(jnp.where(face_perm[:, :, None] == count[None, None, :], count[No...  1.28 us

profile of v1, /device:TPU:0, one launch (start us, length us, event | category | flops | bytes accessed | tf_op | source)
XLA Modules:
  0.0 53.4 jit_solution(7447422457814429261)
XLA Ops:
  0.6 0.7 %fusion = f32[48]{0:T(128)S(1)} fusion(s32[48]{0:T(128)} %param.22, s32[48,1]{0,1:T(1,128)} %param.21), kind=kLoop, calls=%fused_computation.6 | loop fusion | flops 144 | bytes 576 | tf_op jit(solution)/shard_map/convert_element_type | solution.py:393
  1.3 1.3 %copy.17.eig = f32[32,1]{1,0:T(8,128)} copy(f32[32,1]{0,1:T(1,128)} %bitcast.5) | data formatting | bytes 256 | tf_op jit(solution)/shard_map/broadcast_in_dim | solution.py:453
  2.6 1.3 %select_reduce_fusion = s32[48,64]{1,0:T(8,128)S(1)} fusion(s32[48,64]{1,0:T(8,128)} %param.18), kind=kLoop, calls=%fused_computation | loop fusion | flops 586752 | bytes 24576 | tf_op jit(solution)/shard_map/reduce_sum | solution.py:391
  3.9 1.4 %pad_add_fusion.idx = s32[48,128]{1,0:T(8,128)} fusion(s32[48,64]{1,0:T(8,128)} %param.18, s32[48,64]{1,0:T(8,128)S(1)} %broadcast_add_fusion), kind=kLoop, calls=%fused_computation.2 | loop fusion | flops 6144 | bytes 49152 | tf_op jit(solution)/shard_map/concatenate | solution.py:392
  5.4 0.7 %fusion.1 = (f32[32,64]{1,0:T(8,128)S(1)}, f32[32,64]{1,0:T(8,128)S(1)}) fusion(f32[64,64]{1,0:T(8,128)} %pot.1), kind=kLoop, calls=%fused_computation.7 | loop fusion | bytes 32768 | tf_op jit(solution)/shard_map/slice | solution.py:396
  6.1 0.7 %pad_maximum_fusion.early = f32[40,128]{1,0:T(8,128)} fusion(f32[8,128]{1,0:T(8,128)S(1)} %broadcast_in_dim.27, f32[32,64]{1,0:T(8,128)S(1)} %get-tuple-element.4, f32[32,64]{1,0:T(8,128)S(1)} %get-tuple-element.3), kind=kLoop, calls=%fused_computation.3 | loop fusion | flops 10240 | bytes 40960 | tf_op jit(solution)/shard_map/concatenate | solution.py:395
  6.8 1.6 %copy.18.restrict = bf16[512,64]{1,0:T(8,128)(2,1)} copy(bf16[512,64]{0,1:T(8,128)(2,1)} %param.19) | data formatting | bytes 131072 | tf_op args[7]
  8.4 40.4 %shard_map.139 = (bf16[48,32,512]{2,1,0:T(8,128)(2,1)}, f32[64,64]{1,0:T(8,128)}, bf16[48,32,512]{2,1,0:T(8,128)(2,1)}) custom-call(bf16[48,32,512]{2,1,0:T(8,128)(2,1)} %psi.1, bf16[48,32,512]{2,1,0:T(8,128)(2,1)} %src.1, f32[32,1]{1,0:T(8,128)} %copy.17.eig, f32[48]{0:T(128)} %scale.1, f32[48,512]{1,0:T(8,128)} %base.1, bf16[512,512]{1,0:T(8,128)(2,1)} %stiff.1, ...), custom_call_target="tpu_custom_call" | custom-call | tf_op jit(solution)/shard_map/pallas_call | solution.py:403
  48.8 0.0 copy-start.1
  48.8 0.0 copy-start
  48.8 2.8 %copy.22 = bf16[48,32,512]{2,1,0:T(8,128)(2,1)} copy(bf16[48,32,512]{2,1,0:T(8,128)(2,1)} %get-tuple-element.8) | data formatting | bytes 3145728
  51.7 0.0 copy-done.1
  51.7 0.6 %copy.23 = f32[64,64]{1,0:T(8,128)} copy(f32[64,64]{1,0:T(8,128)S(1)} %copy-done.1) | data formatting | bytes 32768
  52.3 0.0 copy-done
  52.3 1.1 %copy.24 = bf16[48,32,512]{2,1,0:T(8,128)(2,1)} copy(bf16[48,32,512]{2,1,0:T(8,128)(2,1)S(1)} %copy-done) | data formatting | bytes 3145728
  (3 shorter events, 0.0 us)
Async XLA Ops:
  48.8 2.9 %copy-start.1 = (f32[64,64]{1,0:T(8,128)S(1)}, f32[64,64]{1,0:T(8,128)}, u32[]{:S(2)}) copy-start(f32[64,64]{1,0:T(8,128)} %get-tuple-element.9) | copy-start | bytes 49156
  48.8 3.5 %copy-start = (bf16[48,32,512]{2,1,0:T(8,128)(2,1)S(1)}, bf16[48,32,512]{2,1,0:T(8,128)(2,1)}, u32[]{:S(2)}) copy-start(bf16[48,32,512]{2,1,0:T(8,128)(2,1)} %get-tuple-element.10) | copy-start | bytes 4718596

commit v2 on v1

--- a/solution.py
+++ b/solution.py
@@ -31,23 +31,35 @@
     return lax.dot_general(a, b, (((0,), (0,)), ((), ())), preferred_element_type=F32)
 
 
+def dot_last(a, b):
+    return lax.dot_general(a, b, (((1,), (1,)), ((), ())), preferred_element_type=F32)
+
+
 def kernel(
     n,
     ranks,
-    psi,
-    src,
-    eig,
+    psi_any,
+    src_any,
+    eigs,
     scale,
     base,
     stiff,
-    idx,
-    early,
+    perm,
+    owner,
+    slots,
     restrict,
     prolong,
     pot,
+    adj_any,
+    upd,
+    app_any,
+    psi,
+    src,
     adj,
-    upd,
     app,
+    idx,
+    eig,
+    early,
     it,
     kin,
     face0,
@@ -83,8 +95,12 @@
     pr,
     ws,
     wr,
+    ins,
+    outs,
 ):
     cells, orbs, nodes = psi.shape
+    end = cells - 1
+    faces = perm.shape[1]
     half = cells // 2
     prow = pot.shape[0]
     phalf = prow // 2
@@ -93,6 +109,14 @@
     d = lax.axis_index("dom")
     r = lax.axis_index("orb")
     barrier = pltpu.get_barrier_semaphore()
+    src_copies = [
+        pltpu.make_async_copy(src_any.at[pl.ds(a, m)], src.at[pl.ds(a, m)], ins.at[k])
+        for k, (a, m) in enumerate(((0, 1), (end, 1), (1, end - 1)))
+    ]
+    psi_copy = pltpu.make_async_copy(psi_any, psi, ins.at[3])
+    for copy in src_copies:
+        copy.start()
+    psi_copy.start()
 
     def greet_dom(k, carry):
         pl.semaphore_signal(barrier, inc=1, device_id={"dom": lax.rem(d + k, n)}, device_id_type=pl.DeviceIdType.MESH)
@@ -146,11 +170,25 @@
 
     group = 8 if cells % 8 == 0 else 1
 
-    def init(c, carry):
-        it[c] = relax * src[c].astype(F32)
-        return carry
-
-    lax.fori_loop(0, cells, init, 0, unroll=4)
+    row0 = lax.broadcasted_iota(jnp.int32, (orbs, 1), 0)
+    column = jnp.zeros((orbs, 1), F32)
+    for o in range(orbs):
+        column = jnp.where(row0 == o, eigs[o], column)
+    eig[...] = column
+    lane1 = lax.broadcasted_iota(jnp.int32, (1, LANES), 1)
+    tcols[...] = jnp.zeros_like(tcols)
+    tcols[:cells, :faces] = perm[...].astype(F32)
+    tturn[...] = jnp.transpose(tcols[...])
+    place = lax.broadcasted_iota(jnp.int32, (faces, LANES), 0).astype(F32)
+    inverse = jnp.zeros((faces, LANES), F32)
+    for k in range(faces):
+        inverse = jnp.where(place == tturn[k : k + 1, :], float(k), inverse)
+    tturn[:faces] = inverse
+    tturn[faces:] = tturn[faces:] * 0.0
+    inverse = jnp.transpose(tturn[...])[:cells]
+    lanes = lax.broadcasted_iota(jnp.int32, (cells, LANES), 1)
+    both = jnp.where(lanes < faces, inverse + faces, pltpu.roll(tcols[:cells], faces, 1))
+    idx[...] = both.astype(jnp.int32)
 
     def apply_group(g, carry):
         block = psi[pl.ds(g * group, group)].astype(F32).reshape(group * orbs, nodes).astype(BF16)
@@ -161,12 +199,13 @@
             kin[c] = scale[c] * part + base[pl.ds(c, 1), :] * psi[c].astype(F32)
         return carry
 
-    def step_group(g, carry):
-        block = it[pl.ds(g * group, group)].reshape(group * orbs, nodes).astype(BF16)
+    def step_group(first, g, carry):
+        block = relax * src[pl.ds(g * group, group)].astype(F32) if first else it[pl.ds(g * group, group)]
+        block = block.reshape(group * orbs, nodes).astype(BF16)
         product = dot(block, stiff[...])
         for k in range(group):
             c = g * group + k
-            value = it[c]
+            value = relax * src[c].astype(F32) if first else it[c]
             part = scale[c] * product[k * orbs : (k + 1) * orbs] + (base[pl.ds(c, 1), :] - eig[...]) * value
             it[c] = value + relax * (src[c].astype(F32) - part)
             face0[c] = part[:, :LANES]
@@ -179,15 +218,22 @@
         it[c, :, last:] = it[c, :, last:] - relax * jnp.where(low, 0.0, y)
         return carry
 
-    end = cells - 1
     shares = -(-(n - 1) // max(1, ITERS - 1))
     for t in range(ITERS):
-        edge = it[0]
+        if t == 0:
+            src_copies[0].wait()
+            src_copies[1].wait()
+        edge = relax * src[0].astype(F32) if t == 0 else it[0]
         tx_l[t] = scale[0] * dot(edge.astype(BF16), stiff[:, :LANES]) + (base[0:1, :LANES] - eig[...]) * edge[:, :LANES]
-        edge = it[end]
+        edge = relax * src[end].astype(F32) if t == 0 else it[end]
         part = scale[end] * dot(edge.astype(BF16), stiff[:, last:]) + (base[end : end + 1, last:] - eig[...]) * edge[:, last:]
         tx_r[t] = turned(part, idx[end : end + 1, :])
         if t == 0:
+            row = jnp.zeros((1, LANES), jnp.int32)
+            for c in range(cells):
+                row = jnp.where(lane1 == c, owner[c] * prow + slots[c], row)
+            early[:phalf] = jnp.concatenate([pot[:phalf], pot[phalf:]], axis=1)
+            early[phalf:] = jnp.broadcast_to(row.astype(F32), (8, LANES))
             pl.semaphore_wait(barrier, n - 1 + ranks - 1)
 
         @pl.when(has_left)
@@ -203,9 +249,12 @@
             return carry
 
         lax.fori_loop(min(n, 1 + t * shares), min(n, 1 + (t + 1) * shares), send_early, 0)
-        lax.fori_loop(0, cells // group, step_group, 0)
+        if t == 0:
+            src_copies[2].wait()
+        lax.fori_loop(0, cells // group, functools.partial(step_group, t == 0), 0)
         lax.fori_loop(0, end, inner_face, 0, unroll=2)
         if t == 0:
+            psi_copy.wait()
             lax.fori_loop(0, cells // group, apply_group, 0)
             ex_tl[:orbs] = kin[0, :, :LANES]
             ex_tl[orbs:] = psi[0].astype(F32)[:, :LANES]
@@ -238,7 +287,7 @@
 
     lax.fori_loop(0, cells, finish, 0, unroll=2)
     d_hi, d_lo = split(dens[...])
-    projected = dot(d_hi, restrict[...]) + dot(d_lo, restrict[...])
+    projected = dot_last(d_hi, restrict[...]) + dot_last(d_lo, restrict[...])
     rows = jnp.concatenate([projected[:half], projected[half:]], axis=1)
     own[...] = rows
     rows_all[d] = rows
@@ -254,6 +303,8 @@
         return carry
 
     lax.fori_loop(0, cells, store, 0, unroll=2)
+    adj_copy = pltpu.make_async_copy(adj, adj_any, outs.at[cells // group])
+    adj_copy.start()
     early_all[d] = early[...]
 
     def wait_early(k, carry):
@@ -270,8 +321,6 @@
 
     lax.fori_loop(0, n, take_row, 0)
     tturn[...] = jnp.transpose(tcols[...])
-    lane1 = lax.broadcasted_iota(jnp.int32, (1, LANES), 1)
-
     def spot(e, at):
         row = early_all[e, phalf : phalf + 1, :]
         return jnp.sum(jnp.where(lane1 == at, row, 0.0), axis=1, keepdims=True)
@@ -328,8 +377,6 @@
         ).astype(BF16)
         return carry
 
-    lax.fori_loop(0, cells, middle, 0, unroll=4)
-
     def joint(c, carry):
         t0, t3 = value0(c + 1), value3(c)
         y = turned(jnp.where(low, t0, t3), idx[pl.ds(c, 1), :])
@@ -337,7 +384,6 @@
         app[c, :, last:] = (t3 + jnp.where(low, 0.0, y)).astype(BF16)
         return carry
 
-    lax.fori_loop(0, end, joint, 0, unroll=2)
     app[0, :, :LANES] = value0(0).astype(BF16)
     app[end, :, last:] = value3(end).astype(BF16)
 
@@ -355,6 +401,14 @@
         y = turned(far, idx[end : end + 1, :])
         app[end, :, last:] = (value3(end) + jnp.where(low, 0.0, y)).astype(BF16)
 
+    app_copies = []
+    for g in range(cells // group):
+        lax.fori_loop(g * group, (g + 1) * group, middle, 0, unroll=2)
+        lax.fori_loop(g * group, min(end, (g + 1) * group), joint, 0, unroll=2)
+        spread_of = pl.ds(g * group, group)
+        app_copies.append(pltpu.make_async_copy(app.at[spread_of], app_any.at[spread_of], outs.at[g]))
+        app_copies[g].start()
+
     @pl.when(has_left)
     def _():
         x_left.wait_send()
@@ -366,6 +420,10 @@
         x_right.wait_send()
         for t in range(ITERS):
             to_right(t).wait_send()
+
+    adj_copy.wait()
+    for copy in app_copies:
+        copy.wait()
 
 
 def local(
@@ -385,18 +443,10 @@
     potential,
 ):
     cells, orbs, nodes = orbitals.shape
-    faces = face_perm.shape[1]
-    prow, coarse = potential.shape
-    count = jnp.arange(faces, dtype=jnp.int32)
-    inverse = jnp.sum(jnp.where(face_perm[:, :, None] == count[None, None, :], count[None, :, None], 0), axis=1)
-    idx = jnp.concatenate([inverse + faces, face_perm], axis=1)
-    target = (owner[:, 0] * prow + pot_slot).astype(F32)
-    target = jnp.broadcast_to(jnp.pad(target, (0, LANES - cells))[None], (8, LANES))
-    early = jnp.concatenate(
-        [jnp.concatenate([potential[: prow // 2], potential[prow // 2 :]], axis=1), target], axis=0
-    )
+    prow = potential.shape[0]
     vmem = pl.BlockSpec(memory_space=pltpu.VMEM)
     smem = pl.BlockSpec(memory_space=pltpu.SMEM)
+    hbm = pl.BlockSpec(memory_space=pl.ANY)
     dma = pltpu.SemaphoreType.DMA
     half = cells // 2
     face = (orbs, LANES)
@@ -407,9 +457,16 @@
             jax.ShapeDtypeStruct(potential.shape, F32),
             jax.ShapeDtypeStruct(orbitals.shape, BF16),
         ),
-        in_specs=[vmem, vmem, vmem, smem, vmem, vmem, vmem, vmem, vmem, vmem, vmem],
-        out_specs=(vmem, vmem, vmem),
+        in_specs=[hbm, hbm, smem, smem, vmem, vmem, vmem, smem, smem, vmem, vmem, vmem],
+        out_specs=(hbm, vmem, hbm),
         scratch_shapes=[
+            pltpu.VMEM((cells, orbs, nodes), BF16),
+            pltpu.VMEM((cells, orbs, nodes), BF16),
+            pltpu.VMEM((cells, orbs, nodes), BF16),
+            pltpu.VMEM((cells, orbs, nodes), BF16),
+            pltpu.VMEM((cells, LANES), jnp.int32),
+            pltpu.VMEM((orbs, 1), F32),
+            pltpu.VMEM((prow // 2 + 8, LANES), F32),
             pltpu.VMEM((cells, orbs, nodes), F32),
             pltpu.VMEM((cells, orbs, nodes), F32),
             pltpu.VMEM((cells,) + face, F32),
@@ -445,18 +502,21 @@
             dma((n,)),
             dma((ranks,)),
             dma((ranks,)),
+            dma((4,)),
+            dma((cells + 1,)),
         ],
         compiler_params=pltpu.CompilerParams(collective_id=0, has_side_effects=True),
     )(
         orbitals,
         adjoint_source,
-        eigenvalues[:, None],
+        eigenvalues,
         cell_scale,
         base_potential,
         stiffness,
-        idx,
-        early,
-        restrict,
+        face_perm,
+        owner[:, 0],
+        pot_slot,
+        restrict.T,
         prolong,
         potential,
     )

time: 53.9 us -> 45.3 us (0.84)
  other arithmetic: 4.07 us -> 0 us
  local copies, waits for them, and re-layouts: 8.29 us -> 4.61 us
    concatenate x2 -> x0, other arithmetic: 2.11 us -> none  [the longest x1 1.43 us: local(): idx = jnp.concatenate([inverse + faces, face_perm], axis=1)]
    unnamed x8 -> x7, local copies, waits for them, and re-layouts: 6.21 us -> 4.61 us
    broadcast_in_dim x2 -> x0, local copies, waits for them, and re-layouts: 1.33 us -> none  [the longest x1 1.33 us: local(): eigenvalues[:, None]]
    reduce_sum x1 -> x0, other arithmetic: 1.28 us -> none  [local(): jnp.sum(jnp.where(face_perm[:, :, None] == count[None, None, :], count[No...]
    slice x1 -> x0, local copies, waits for them, and re-layouts: 0.74 us -> none  [local(): potential[:prow // 2]]
    convert_element_type x1 -> x0, other arithmetic: 0.68 us -> none  [local(): target = (owner[:, 0] * prow + pot_slot).astype(F32)]
    pallas_call x1, Pallas kernels: 40.4 us -> 39.9 us  [local(): pl.pallas_call(functools.partial(kernel, n, ranks), out_shape=(jax.ShapeD...]
where the time goes in v2:
time: 45.3 us; the launch traced here: 45.1 us
  Pallas kernels  39.9 us (88%)
  local copies, waits for them, and re-layouts  4.61 us (10%)
  between operations  0.66 us (1%)
    pallas_call x1, Pallas kernels, local(): pl.pallas_call(functools.partial(kernel, n, ranks), out_shape=(jax.ShapeD...  39.9 us
    unnamed x7, local copies, waits for them, and re-layouts  4.61 us

profile of v2, /device:TPU:0, one launch (start us, length us, event | category | flops | bytes accessed | tf_op | source)
XLA Modules:
  0.0 45.1 jit_solution(8471431609302335241)
XLA Ops:
  0.6 39.9 %shard_map.139 = (bf16[48,32,512]{2,1,0:T(8,128)(2,1)}, f32[64,64]{1,0:T(8,128)}, bf16[48,32,512]{2,1,0:T(8,128)(2,1)}) custom-call(bf16[48,32,512]{2,1,0:T(8,128)(2,1)} %psi_any.1, bf16[48,32,512]{2,1,0:T(8,128)(2,1)} %src_any.1, f32[32]{0:T(128)} %eigs.1, f32[48]{0:T(128)} %scale.1, f32[48,512]{1,0:T(8,128)} %base.1, bf16[512,512]{1,0:T(8,128)(2,1)} %stiff.1, ...), custom_call_target="tpu_custom_call" | custom-call | tf_op jit(solution)/shard_map/pallas_call | solution.py:453
  40.5 0.0 copy-start.1
  40.5 0.0 copy-start
  40.5 2.8 %copy.18 = bf16[48,32,512]{2,1,0:T(8,128)(2,1)} copy(bf16[48,32,512]{2,1,0:T(8,128)(2,1)} %get-tuple-element.6) | data formatting | bytes 3145728
  43.4 0.0 copy-done.1
  43.4 0.6 %copy.19 = f32[64,64]{1,0:T(8,128)} copy(f32[64,64]{1,0:T(8,128)S(1)} %copy-done.1) | data formatting | bytes 32768
  44.0 0.0 copy-done
  44.0 1.1 %copy.20 = bf16[48,32,512]{2,1,0:T(8,128)(2,1)} copy(bf16[48,32,512]{2,1,0:T(8,128)(2,1)S(1)} %copy-done) | data formatting | bytes 3145728
Async XLA Ops:
  40.5 2.9 %copy-start.1 = (f32[64,64]{1,0:T(8,128)S(1)}, f32[64,64]{1,0:T(8,128)}, u32[]{:S(2)}) copy-start(f32[64,64]{1,0:T(8,128)} %get-tuple-element.7) | copy-start | bytes 49156
  40.5 3.5 %copy-start = (bf16[48,32,512]{2,1,0:T(8,128)(2,1)S(1)}, bf16[48,32,512]{2,1,0:T(8,128)(2,1)}, u32[]{:S(2)}) copy-start(bf16[48,32,512]{2,1,0:T(8,128)(2,1)} %get-tuple-element.8) | copy-start | bytes 4718596

commit v3 on v2

--- a/solution.py
+++ b/solution.py
@@ -50,13 +50,11 @@
     restrict,
     prolong,
     pot,
-    adj_any,
+    adj,
     upd,
-    app_any,
+    app,
     psi,
     src,
-    adj,
-    app,
     idx,
     eig,
     early,
@@ -96,7 +94,6 @@
     ws,
     wr,
     ins,
-    outs,
 ):
     cells, orbs, nodes = psi.shape
     end = cells - 1
@@ -212,10 +209,17 @@
             face3[c] = part[:, last:]
         return carry
 
-    def inner_face(c, carry):
-        y = turned(jnp.where(low, face0[c + 1], face3[c]), idx[pl.ds(c, 1), :])
-        it[c + 1, :, :LANES] = it[c + 1, :, :LANES] - relax * jnp.where(low, y, 0.0)
-        it[c, :, last:] = it[c, :, last:] - relax * jnp.where(low, 0.0, y)
+    def inner_faces(start, count):
+        at = [start + k for k in range(count)]
+        ys = [turned(jnp.where(low, face0[c + 1], face3[c]), idx[pl.ds(c, 1), :]) for c in at]
+        lefts = [it[c + 1, :, :LANES] for c in at]
+        rights = [it[c, :, last:] for c in at]
+        for c, y, a, b in zip(at, ys, lefts, rights):
+            it[c + 1, :, :LANES] = a - relax * jnp.where(low, y, 0.0)
+            it[c, :, last:] = b - relax * jnp.where(low, 0.0, y)
+
+    def inner_group(g, carry):
+        inner_faces(g * group, group)
         return carry
 
     shares = -(-(n - 1) // max(1, ITERS - 1))
@@ -252,7 +256,9 @@
         if t == 0:
             src_copies[2].wait()
         lax.fori_loop(0, cells // group, functools.partial(step_group, t == 0), 0)
-        lax.fori_loop(0, end, inner_face, 0, unroll=2)
+        lax.fori_loop(0, end // group, inner_group, 0)
+        if end % group:
+            inner_faces(end - end % group, end % group)
         if t == 0:
             psi_copy.wait()
             lax.fori_loop(0, cells // group, apply_group, 0)
@@ -285,7 +291,7 @@
         dens[pl.ds(c, 1), :] = jnp.sum(psi[c].astype(F32) * it[c], axis=0, keepdims=True)
         return carry
 
-    lax.fori_loop(0, cells, finish, 0, unroll=2)
+    lax.fori_loop(0, cells, finish, 0, unroll=4)
     d_hi, d_lo = split(dens[...])
     projected = dot_last(d_hi, restrict[...]) + dot_last(d_lo, restrict[...])
     rows = jnp.concatenate([projected[:half], projected[half:]], axis=1)
@@ -302,9 +308,7 @@
         adj[c] = it[c].astype(BF16)
         return carry
 
-    lax.fori_loop(0, cells, store, 0, unroll=2)
-    adj_copy = pltpu.make_async_copy(adj, adj_any, outs.at[cells // group])
-    adj_copy.start()
+    lax.fori_loop(0, cells, store, 0, unroll=4)
     early_all[d] = early[...]
 
     def wait_early(k, carry):
@@ -377,11 +381,16 @@
         ).astype(BF16)
         return carry
 
-    def joint(c, carry):
-        t0, t3 = value0(c + 1), value3(c)
-        y = turned(jnp.where(low, t0, t3), idx[pl.ds(c, 1), :])
-        app[c + 1, :, :LANES] = (t0 + jnp.where(low, y, 0.0)).astype(BF16)
-        app[c, :, last:] = (t3 + jnp.where(low, 0.0, y)).astype(BF16)
+    def joints(start, count):
+        at = [start + k for k in range(count)]
+        pairs = [(value0(c + 1), value3(c)) for c in at]
+        ys = [turned(jnp.where(low, t0, t3), idx[pl.ds(c, 1), :]) for c, (t0, t3) in zip(at, pairs)]
+        for c, (t0, t3), y in zip(at, pairs, ys):
+            app[c + 1, :, :LANES] = (t0 + jnp.where(low, y, 0.0)).astype(BF16)
+            app[c, :, last:] = (t3 + jnp.where(low, 0.0, y)).astype(BF16)
+
+    def joint_group(g, carry):
+        joints(g * group, group)
         return carry
 
     app[0, :, :LANES] = value0(0).astype(BF16)
@@ -401,13 +410,10 @@
         y = turned(far, idx[end : end + 1, :])
         app[end, :, last:] = (value3(end) + jnp.where(low, 0.0, y)).astype(BF16)
 
-    app_copies = []
-    for g in range(cells // group):
-        lax.fori_loop(g * group, (g + 1) * group, middle, 0, unroll=2)
-        lax.fori_loop(g * group, min(end, (g + 1) * group), joint, 0, unroll=2)
-        spread_of = pl.ds(g * group, group)
-        app_copies.append(pltpu.make_async_copy(app.at[spread_of], app_any.at[spread_of], outs.at[g]))
-        app_copies[g].start()
+    lax.fori_loop(0, cells, middle, 0, unroll=4)
+    lax.fori_loop(0, end // group, joint_group, 0)
+    if end % group:
+        joints(end - end % group, end % group)
 
     @pl.when(has_left)
     def _():
@@ -420,10 +426,6 @@
         x_right.wait_send()
         for t in range(ITERS):
             to_right(t).wait_send()
-
-    adj_copy.wait()
-    for copy in app_copies:
-        copy.wait()
 
 
 def local(
@@ -453,15 +455,13 @@
     return pl.pallas_call(
         functools.partial(kernel, n, ranks),
         out_shape=(
-            jax.ShapeDtypeStruct(orbitals.shape, BF16),
-            jax.ShapeDtypeStruct(potential.shape, F32),
-            jax.ShapeDtypeStruct(orbitals.shape, BF16),
+            pltpu.VMEM(orbitals.shape, BF16),
+            pltpu.VMEM(potential.shape, F32),
+            pltpu.VMEM(orbitals.shape, BF16),
         ),
         in_specs=[hbm, hbm, smem, smem, vmem, vmem, vmem, smem, smem, vmem, vmem, vmem],
-        out_specs=(hbm, vmem, hbm),
+        out_specs=(vmem, vmem, vmem),
         scratch_shapes=[
-            pltpu.VMEM((cells, orbs, nodes), BF16),
-            pltpu.VMEM((cells, orbs, nodes), BF16),
             pltpu.VMEM((cells, orbs, nodes), BF16),
             pltpu.VMEM((cells, orbs, nodes), BF16),
             pltpu.VMEM((cells, LANES), jnp.int32),
@@ -503,7 +503,6 @@
             dma((ranks,)),
             dma((ranks,)),
             dma((4,)),
-            dma((cells + 1,)),
         ],
         compiler_params=pltpu.CompilerParams(collective_id=0, has_side_effects=True),
     )(

time: 45.3 us -> 38.5 us (0.85)
  Pallas kernels: 39.9 us -> 34.8 us
  local copies, waits for them, and re-layouts: 4.61 us -> 2.9 us
    pallas_call x1, Pallas kernels: 39.9 us -> 34.8 us  [local(): pl.pallas_call(functools.partial(kernel, n, ranks), out_shape=(pltpu.VMEM...]
    unnamed x7 -> x3, local copies, waits for them, and re-layouts: 4.61 us -> 2.9 us
where the time goes in v3:
time: 38.5 us; the launch traced here: 38.4 us
  Pallas kernels  34.8 us (90%)
  local copies, waits for them, and re-layouts  2.9 us (8%)
  between operations  0.64 us (2%)
    pallas_call x1, Pallas kernels, local(): pl.pallas_call(functools.partial(kernel, n, ranks), out_shape=(pltpu.VMEM...  34.8 us
    unnamed x3, local copies, waits for them, and re-layouts  2.9 us

profile of v3, /device:TPU:0, one launch (start us, length us, event | category | flops | bytes accessed | tf_op | source)
XLA Modules:
  0.0 38.4 jit_solution(11477382335688984359)
XLA Ops:
  0.6 34.8 %shard_map.139 = (bf16[48,32,512]{2,1,0:T(8,128)(2,1)S(1)}, f32[64,64]{1,0:T(8,128)S(1)}, bf16[48,32,512]{2,1,0:T(8,128)(2,1)S(1)}) custom-call(bf16[48,32,512]{2,1,0:T(8,128)(2,1)} %psi_any.1, bf16[48,32,512]{2,1,0:T(8,128)(2,1)} %src_any.1, f32[32]{0:T(128)} %eigs.1, f32[48]{0:T(128)} %scale.1, f32[48,512]{1,0:T(8,128)} %base.1, bf16[512,512]{1,0:T(8,128)(2,1)} %stiff.1, ...), custom_call_target="tpu_custom_call" | custom-call | tf_op jit(solution)/shard_map/pallas_call | solution.py:455
  35.5 1.1 %copy.18 = bf16[48,32,512]{2,1,0:T(8,128)(2,1)} copy(bf16[48,32,512]{2,1,0:T(8,128)(2,1)S(1)} %get-tuple-element.3) | data formatting | bytes 3145728
  36.6 0.6 %copy.19 = f32[64,64]{1,0:T(8,128)} copy(f32[64,64]{1,0:T(8,128)S(1)} %get-tuple-element.4) | data formatting | bytes 32768
  37.2 1.1 %copy.20 = bf16[48,32,512]{2,1,0:T(8,128)(2,1)} copy(bf16[48,32,512]{2,1,0:T(8,128)(2,1)S(1)} %get-tuple-element.5) | data formatting | bytes 3145728
